TPU v7x, 32 devices: a whole 2x2x4 slice. The times are simulated.
32 devices in a mesh: wide: 8 (over z, y), narrow: 4 (over x, core).
Axes of the slice: x: 2, y: 2, z: 4, core: 2. Of those that a mesh axis runs over, the one named last changes fastest.
Arguments:
- activations: bfloat16 [256, 28672], P('wide', 'narrow'), may hold values from -6 to 6
- out_grads: bfloat16 [256, 8192], P('wide'), may hold values from -6 to 6
- basis_in: bfloat16 [28672, 28672], P('narrow', 'wide'), may hold values from -0.03125 to 0.03125
- basis_out: bfloat16 [8192, 8192], P('wide', 'narrow'), may hold values from -0.0625 to 0.0625
- eigenvalues: bfloat16 [8192, 28672], P('narrow', 'wide'), may hold values from 0.29882812 to 10
- queries: bfloat16 [2, 8192, 28672], P(None, 'narrow', 'wide'), may hold values from -0.00036621094 to 0.00036621094
- doc_ids: int32 [256], replicated, may hold values from 0 to 15, never falling along the last dimension, each value on 1 to 32 neighbouring positions
Outputs:
- scores: float32 [16, 2], replicated
Inputs may be any that keep to these rules, and one draw needn't show every extreme that they name: `doc_ids`: document numbers never fall along the tokens; each document has 1 to 32 tokens.
All inputs are finite; a program needn't handle non-finite values.
Results may differ from a plain program's by a relative error of at most 0.0051.
Values may be sent and summed in bfloat16 or wider, within the bound.
A program may use at most 192 MiB of HBM per device.

v0:
```python
import jax
import jax.numpy as jnp
from jax import lax
from jax.sharding import PartitionSpec as P

DOC_PER = 2


DAMPING = 0.1


def shards(activations, out_grads, basis_in, basis_out, eigenvalues, queries, doc_ids):
    partial_acts = jnp.dot(
        lax.all_gather(activations, "wide", axis=0, tiled=True),
        basis_in,
        preferred_element_type=jnp.float32,
    )
    rot_acts = lax.psum(partial_acts, "narrow").astype(jnp.bfloat16)
    rows_held = lax.all_to_all(out_grads, "wide", split_axis=1, concat_axis=0, tiled=True)
    partial_grads = jnp.dot(rows_held, basis_out, preferred_element_type=jnp.float32)
    rot_grads = lax.psum(partial_grads, "wide").astype(jnp.bfloat16)
    precond = (
        queries.astype(jnp.float32) / (eigenvalues.astype(jnp.float32)[None] + DAMPING)
    ).astype(jnp.bfloat16)
    mixed_rows = jnp.einsum("ti,qij->qtj", rot_grads, precond, preferred_element_type=jnp.float32)
    token_part = jnp.sum(mixed_rows * rot_acts.astype(jnp.float32)[None], axis=2)
    doc_count = DOC_PER * lax.axis_size("wide")
    member = (doc_ids[None, :] == jnp.arange(doc_count, dtype=jnp.int32)[:, None]).astype(
        jnp.float32
    )
    partial_docs = jnp.dot(member, token_part.T, precision=lax.Precision.HIGHEST)
    return lax.psum(partial_docs, ("wide", "narrow"))


def solution(mesh):
    return jax.shard_map(
        shards,
        mesh=mesh,
        in_specs=(
            P("wide", "narrow"),
            P("wide", None),
            P("narrow", "wide"),
            P("wide", "narrow"),
            P("narrow", "wide"),
            P(None, "narrow", "wide"),
            P(),
        ),
        out_specs=P(),
        check_vma=False,
    )
```

profile of v0, /device:TPU:0, one launch (start us, length us, event | category | flops | bytes accessed | tf_op | source)
XLA Modules:
  0.0 313.1 jit_solution(6194928226690925329)
XLA Ops:
  6.5 0.0 all-gather.2.cloned.1.call-start
  6.5 0.7 all-gather.2.cloned.1.call-update
  7.3 1.9 copy.17
  9.1 7.3 %all-to-all-start = ((bf16[32,8,1024]{2,0,1:T(8,128)(2,1)}), bf16[32,8,1024]{2,0,1:T(8,128)(2,1)S(1)}, u32[]{:S(2)}, u32[]{:S(2)}) async-start(bf16[32,8,1024]{2,0,1:T(8,128)(2,1)} %bitcast.18), calls=%async_computation | async-start | bytes 1048576 | tf_op jit(solution)/shard_map/all_to_all | solution.py:19
  16.4 16.8 %convert_add_fusion = f32[2048,3584]{1,0:T(8,128)} fusion(bf16[2048,3584]{1,0:T(8,128)(2,1)} %param.11), kind=kLoop, calls=%fused_computation.1 | loop fusion | flops 14680064 | bytes 44040192 | tf_op jit(solution)/shard_map/add | solution.py:23
  33.3 7.1 %all-to-all-done = bf16[32,8,1024]{2,0,1:T(8,128)(2,1)S(1)} async-done(((bf16[32,8,1024]{2,0,1:T(8,128)(2,1)}), bf16[32,8,1024]{2,0,1:T(8,128)(2,1)S(1)}, u32[]{:S(2)}, u32[]{:S(2)}) %all-to-all-start) | async-done | bytes 524320 | tf_op jit(solution)/shard_map/all_to_all | solution.py:19
  40.4 3.5 %fusion.6 = f32[256,2048]{1,0:T(8,128)S(1)} fusion(bf16[256,1024]{1,0:T(8,128)(2,1)S(1)} %bitcast.20, bf16[1024,2048]{1,0:T(8,128)(2,1)} %param.10), kind=kOutput, calls=%fused_computation.12 | convolution fusion | flops 1073741824 | bytes 6815744 | tf_op jit(solution)/shard_map/dot_general | solution.py:20
  43.8 109.9 %all-reduce.3 = bf16[256,2048]{1,0:T(8,128)(2,1)S(1)} all-reduce(f32[256,2048]{1,0:T(8,128)S(1)} %fusion.6), channel_id=1, replica_groups=mesh['wide'=8,'narrow'=4] {'wide'}, use_global_device_ids=true, to_apply=%region_0.0 | all-reduce | flops 524288 | bytes 3145728 | tf_op jit(solution)/shard_map/psum | solution.py:21
  153.7 0.0 all-gather.2.cloned.1.call-done
  153.8 24.1 %fusion.7 = f32[256,3584]{1,0:T(8,128)} fusion(bf16[256,7168]{1,0:T(8,128)(2,1)} %all-gather.2.cloned.1.call-done, bf16[7168,3584]{1,0:T(8,128)(2,1)} %param.9), kind=kOutput, calls=%fused_computation.13 | convolution fusion | flops 13153337344 | bytes 58720256 | tf_op jit(solution)/shard_map/dot_general | solution.py:13
  177.8 67.2 %all-reduce.2 = bf16[256,3584]{1,0:T(8,128)(2,1)S(1)} all-reduce(f32[256,3584]{1,0:T(8,128)} %fusion.7), channel_id=1, replica_groups=mesh['wide'=8,'narrow'=4] {'narrow'}, use_global_device_ids=true, to_apply=%region_1.0 | all-reduce | flops 917504 | bytes 5505024 | tf_op jit(solution)/shard_map/psum | solution.py:18
  245.0 2.8 copy.13
  247.8 0.0 copy-start
  247.8 21.5 %fusion.1 = f32[2,256]{1,0:T(2,128)S(1)} fusion(bf16[2,2048,3584]{2,1,0:T(8,128)(2,1)} %param.12, f32[2048,3584]{1,0:T(8,128)} %convert_add_fusion, f32[256,3584]{0,1:T(8,128)} %copy.13, bf16[256,2048]{1,0:T(8,128)(2,1)S(1)} %all-reduce.3), kind=kOutput, calls=%fused_computation.4 | convolution fusion | flops 7563902464 | bytes 63440896 | tf_op jit(solution)/shard_map/ti,qij->qtj/dot_general | solution.py:25
  269.3 0.0 copy-done
  269.4 0.1 fusion.4
  269.5 36.8 %psum.23 = f32[16,2]{0,1:T(2,128)} all-reduce(f32[16,2]{0,1:T(2,128)S(1)} %fusion.4), channel_id=1, replica_groups=mesh['wide'=8,'narrow'=4] {'wide','narrow'}, use_global_device_ids=true, to_apply=%region_3.0 | all-reduce | flops 32 | bytes 256 | tf_op jit(solution)/shard_map/psum | solution.py:32
Async XLA Ops:
  6.5 147.2 %all-gather.2.cloned.1.call-start = ((), (), s32[]{:S(2)}) async-start(), calls=%async_computation.1 | async-start | bytes 4128768 | tf_op jit(solution)/shard_map/all_gather | solution.py:14
  9.1 31.2 %all-to-all-start = ((bf16[32,8,1024]{2,0,1:T(8,128)(2,1)}), bf16[32,8,1024]{2,0,1:T(8,128)(2,1)S(1)}, u32[]{:S(2)}, u32[]{:S(2)}) async-start(bf16[32,8,1024]{2,0,1:T(8,128)(2,1)} %bitcast.18), calls=%async_computation | async-start | bytes 1048576 | tf_op jit(solution)/shard_map/all_to_all | solution.py:19
  247.8 21.5 %copy-start = (s32[256]{0:T(256)S(1)}, s32[256]{0:T(256)}, u32[]{:S(2)}) copy-start(s32[256]{0:T(256)} %param.13) | copy-start | bytes 3076
Sparse Core Ops, SparseCore 0:
  9.5 118.3 all-gather.1
where the time goes:
time: 314 us; the launch traced here: 313 us
  blocking collectives  214 us (68%)
  matrix products  49.2 us (16%)
  other arithmetic  16.8 us (5%)
  between operations  13.4 us (4%)
  waiting for transfers between devices  7.82 us (2%)
  starting transfers between devices  7.31 us (2%)
  local copies, waits for them, and re-layouts  4.67 us (1%)
    psum x1, blocking collectives, shards(): rot_grads = lax.psum(partial_grads, 'wide').astype(jnp.bfloat16)  110 us
    psum x1, blocking collectives, shards(): rot_acts = lax.psum(partial_acts, 'narrow').astype(jnp.bfloat16)  67.2 us
    psum x1, blocking collectives, shards(): return lax.psum(partial_docs, ('wide', 'narrow'))  36.8 us
    dot_general x1, matrix products, shards(): jnp.dot(lax.all_gather(activations, 'wide', axis=0, tiled=True), basis_in...  24.1 us
    dot_general x1, matrix products, shards(): jnp.einsum('ti,qij->qtj', rot_grads, precond, preferred_element_type=jnp....  21.5 us
    add x1, other arithmetic, shards(): eigenvalues.astype(jnp.float32)[None] + DAMPING  16.8 us
    all_to_all x1, starting transfers between devices, shards(): lax.all_to_all(out_grads, 'wide', split_axis=1, concat_axis=0, tiled=True)  7.31 us
    all_to_all x1, waiting for transfers between devices, shards(): lax.all_to_all(out_grads, 'wide', split_axis=1, concat_axis=0, tiled=True)  7.09 us
  transfers between devices with their start and end apart: 2, of which 1 were waited for; matrix products, arithmetic and copies ran while one was open for 7% of the time, Pallas kernels for 0%

commit v1 on v0

v1 whole, which is shorter than its diff:
```python
import functools

import jax
import jax.numpy as jnp
from jax import lax
from jax.experimental import pallas as pl
from jax.experimental.pallas import tpu as pltpu
from jax.sharding import PartitionSpec as P

DOC_PER = 2
DAMPING = 0.1
F32 = jnp.float32
BF16 = jnp.bfloat16
ANY = pl.BlockSpec(memory_space=pl.ANY)
VMEM_LIMIT = 60 * 1024 * 1024


def tile_of(size, most):
    return max(t for t in range(128, most + 1, 128) if size % t == 0)


def grid_of(wide):
    outer = max(o for o in (1, 2, 3, 4) if wide % o == 0)
    return outer, wide // outer


def remote(src, dst, send, recv, device):
    return pltpu.make_async_remote_copy(
        src_ref=src,
        dst_ref=dst,
        send_sem=send,
        recv_sem=recv,
        device_id=device,
        device_id_type=pl.DeviceIdType.MESH,
    )


def greet(wide, narrow):
    w, n = lax.axis_index("wide"), lax.axis_index("narrow")
    barrier = pltpu.get_barrier_semaphore()
    for d in range(1, wide):
        pl.semaphore_signal(
            barrier, inc=1, device_id={"wide": lax.rem(w + d, wide)}, device_id_type=pl.DeviceIdType.MESH
        )
    for d in range(1, narrow):
        pl.semaphore_signal(
            barrier, inc=1, device_id={"narrow": lax.rem(n + d, narrow)}, device_id_type=pl.DeviceIdType.MESH
        )
    pl.semaphore_wait(barrier, wide + narrow - 2)


def rotate_kernel(
    wide, narrow, acts, grads, basis_in, basis_out, rot_grads, rot_acts,
    acts_all, weights, total, rows_held, weights_out, grads_part, grads_send, first_recv, second_send,
    second_recv, grads_all, acts_send, core_recv, cross_send, cross_recv, acts_done,
    local_sem, weight_sem, out_sem, a2a_s, a2a_r,
    line_s, line_r, side_s, side_r, gline_s, gline_r, gside_s, gside_r,
    first_s, first_r, second_s, second_r, core_s, core_r, cross_s, cross_r, last_s, last_r,
):
    outer, inner = grid_of(wide)
    cross = narrow // 2
    w, n = lax.axis_index("wide"), lax.axis_index("narrow")
    wo, wi = w // inner, lax.rem(w, inner)
    nx, nc = n // 2, lax.rem(n, 2)
    chunks, tokens, depth = acts_all.shape
    block = acts.shape[0]
    columns = total.shape[1]
    rows_out = basis_out.shape[0]
    half = tokens // 2

    def line_peer(d):
        return {"wide": lax.rem(wo + d, outer) * inner + wi}

    def side_peer(e):
        return {"wide": wo * inner + lax.rem(wi + e, inner)}

    def cut(c):
        return pl.ds(pl.multiple_of(c * depth, 128), depth)

    def rows(source):
        return pl.ds(pl.multiple_of(source * block, block), block)

    def line_source(d):
        return lax.rem(wo + outer - d, outer) * inner + wi

    def weight(c):
        slot = lax.rem(c, 2)
        return pltpu.make_async_copy(
            basis_in.at[pl.ds(pl.multiple_of(c * depth, 128), depth)], weights.at[slot], weight_sem.at[slot]
        )

    fetch_out = pltpu.make_async_copy(basis_out, weights_out, local_sem.at[0])
    own_rows = pltpu.make_async_copy(
        grads.at[:, pl.ds(pl.multiple_of(w * rows_out, 128), rows_out)], rows_held.at[rows(w)], local_sem.at[1]
    )

    def own_acts(c):
        return pltpu.make_async_copy(acts.at[:, cut(c)], acts_all.at[c, rows(w)], out_sem.at[c])

    own_rows.start()
    fetch_out.start()
    for c in range(chunks):
        own_acts(c).start()
    weight(0).start()
    weight(1).start()
    greet(wide, narrow)

    def swap(d):
        to = lax.rem(w + d, wide)
        return remote(
            grads.at[:, pl.ds(pl.multiple_of(to * rows_out, 128), rows_out)],
            rows_held.at[rows(w)],
            a2a_s.at[d],
            a2a_r.at[d],
            {"wide": to},
        )

    for d in range(1, wide):
        swap(d).start()

    def line_copy(c, d):
        return remote(
            acts.at[:, cut(c)], acts_all.at[c, rows(w)], line_s.at[c, d], line_r.at[c, d], line_peer(d)
        )

    def side_own(c, e):
        return remote(
            acts.at[:, cut(c)], acts_all.at[c, rows(w)], side_s.at[c, e, 0], side_r.at[c, e, 0], side_peer(e)
        )

    def side_pass(c, e, d):
        source = line_source(d)
        return remote(
            acts_all.at[c, rows(source)],
            acts_all.at[c, rows(source)],
            side_s.at[c, e, d],
            side_r.at[c, e, d],
            side_peer(e),
        )

    def begin(c, carry):
        for d in range(1, outer):
            line_copy(c, d).start()
        for e in range(1, inner):
            side_own(c, e).start()
        return carry

    lax.fori_loop(0, chunks, begin, 0)

    own_rows.wait()
    fetch_out.wait()
    for d in range(1, wide):
        swap(d).wait_recv()
    width = weights_out.shape[1]
    wt = tile_of(width, 512)

    def grads_tile(k, carry):
        at = pl.ds(pl.multiple_of(k * wt, 128), wt)
        part = jnp.dot(rows_held[...], weights_out[:, at], preferred_element_type=F32)
        part = part.reshape(outer, inner, block, wt)
        grads_part[:, :, :, at] = part
        grads_send[:, :, :, at] = part.astype(BF16)
        return carry

    lax.fori_loop(0, width // wt, grads_tile, 0)

    def first(e):
        return remote(
            grads_send.at[:, lax.rem(wi + e, inner)], first_recv.at[e], first_s.at[e], first_r.at[e], side_peer(e)
        )

    for e in range(1, inner):
        first(e).start()

    def second(d):
        return remote(
            second_send.at[lax.rem(wo + d, outer)], second_recv.at[d], second_s.at[d], second_r.at[d], line_peer(d)
        )

    ct = tile_of(columns, 512)

    def forward(c):
        for d in range(1, outer):
            line_copy(c, d).wait_recv()
            for e in range(1, inner):
                side_pass(c, e, d).start()

    def step(c, carry):
        @pl.when(c + 1 < chunks)
        def _():
            forward(c + 1)

        own_acts(c).wait()
        for e in range(1, inner):
            side_own(c, e).wait_recv()
            for d in range(1, outer):
                side_pass(c, e, d).wait_recv()
        weight(c).wait()
        slot = lax.rem(c, 2)

        def tile(k, carry):
            at = pl.ds(pl.multiple_of(k * ct, 128), ct)
            part = jnp.dot(acts_all[c], weights[slot, :, at], preferred_element_type=F32)

            @pl.when(c == 0)
            def _():
                total[:, at] = part

            @pl.when(c > 0)
            def _():
                total[:, at] += part

            return carry

        lax.fori_loop(0, columns // ct, tile, 0)

        @pl.when(c + 2 < chunks)
        def _():
            weight(c + 2).start()

        return carry

    middle = chunks // 2
    forward(0)
    lax.fori_loop(0, middle, step, 0)
    for e in range(1, inner):
        first(e).wait_recv()
    for o in range(outer):
        value = grads_part[o, wi]
        for e in range(1, inner):
            value = value + first_recv[e, o].astype(F32)
        grads_part[o, wi] = value
        second_send[o] = value.astype(BF16)
    for d in range(1, outer):
        second(d).start()
    lax.fori_loop(middle, chunks, step, 0)

    def to_send(k, carry):
        at = pl.ds(pl.multiple_of(k * ct, 128), ct)
        acts_send[:, at] = total[pl.ds(pl.multiple_of((1 - nc) * half, half), half), at].astype(BF16)
        return carry

    lax.fori_loop(0, columns // ct, to_send, 0)
    partner = {"narrow": nx * 2 + (1 - nc)}
    core_copy = remote(acts_send, core_recv, core_s, core_r, partner)
    core_copy.start()

    for d in range(1, outer):
        second(d).wait_recv()
    value = grads_part[wo, wi]
    for d in range(1, outer):
        value = value + second_recv[d].astype(F32)
    grads_all[w] = value.astype(BF16)

    def gline(d):
        return remote(grads_all.at[w], grads_all.at[w], gline_s.at[d], gline_r.at[d], line_peer(d))

    def gside(e, d):
        source = line_source(d)
        return remote(
            grads_all.at[source], grads_all.at[source], gside_s.at[e, d], gside_r.at[e, d], side_peer(e)
        )

    for d in range(1, outer):
        gline(d).start()
    for e in range(1, inner):
        gside(e, 0).start()

    mine = pl.ds(pl.multiple_of(nc * half, half), half)
    core_copy.wait_recv()

    def core_sum(k, carry):
        at = pl.ds(pl.multiple_of(k * ct, 128), ct)
        value = total[mine, at] + core_recv[:, at].astype(F32)
        total[mine, at] = value
        cross_send[:, at] = value.astype(BF16)
        return carry

    lax.fori_loop(0, columns // ct, core_sum, 0)

    def cross_copy(d):
        return remote(
            cross_send, cross_recv.at[d], cross_s.at[d], cross_r.at[d], {"narrow": lax.rem(nx + d, cross) * 2 + nc}
        )

    for d in range(1, cross):
        cross_copy(d).start()
    for d in range(1, outer):
        gline(d).wait_recv()
        for e in range(1, inner):
            gside(e, d).start()
    for d in range(1, cross):
        cross_copy(d).wait_recv()

    def cross_sum(k, carry):
        at = pl.ds(pl.multiple_of(k * ct, 128), ct)
        value = total[mine, at]
        for d in range(1, cross):
            value = value + cross_recv[d, :, at].astype(F32)
        acts_done[nc, :, at] = value.astype(BF16)
        return carry

    lax.fori_loop(0, columns // ct, cross_sum, 0)
    last = remote(acts_done.at[nc], acts_done.at[nc], last_s, last_r, partner)
    last.start()
    for e in range(1, inner):
        for d in range(outer):
            gside(e, d).wait_recv()
    put_grads = pltpu.make_async_copy(grads_all, rot_grads, local_sem.at[0])
    put_grads.start()
    last.wait_recv()
    put_acts = pltpu.make_async_copy(acts_done, rot_acts, local_sem.at[1])
    put_acts.start()

    for d in range(1, wide):
        swap(d).wait_send()

    def drain(c, carry):
        for d in range(1, outer):
            line_copy(c, d).wait_send()
        for e in range(1, inner):
            side_own(c, e).wait_send()
            for d in range(1, outer):
                side_pass(c, e, d).wait_send()
        return carry

    lax.fori_loop(0, chunks, drain, 0)
    for e in range(1, inner):
        first(e).wait_send()
        for d in range(outer):
            gside(e, d).wait_send()
    for d in range(1, outer):
        second(d).wait_send()
        gline(d).wait_send()
    core_copy.wait_send()
    for d in range(1, cross):
        cross_copy(d).wait_send()
    last.wait_send()
    put_grads.wait()
    put_acts.wait()


def rotate(wide, narrow, activations, out_grads, basis_in, basis_out):
    outer, inner = grid_of(wide)
    cross = narrow // 2
    block, depth_all = activations.shape
    tokens = block * wide
    depth = tile_of(depth_all, 1024)
    chunks = depth_all // depth
    columns = basis_in.shape[1]
    rows_out, width = basis_out.shape
    half = tokens // 2
    dma = pltpu.SemaphoreType.DMA
    grads, acts = pl.pallas_call(
        functools.partial(rotate_kernel, wide, narrow),
        out_shape=(
            jax.ShapeDtypeStruct((wide, block, width), BF16),
            jax.ShapeDtypeStruct((2, half, columns), BF16),
        ),
        in_specs=[ANY] * 4,
        out_specs=(ANY, ANY),
        scratch_shapes=[
            pltpu.VMEM((chunks, tokens, depth), BF16),
            pltpu.VMEM((2, depth, columns), BF16),
            pltpu.VMEM((tokens, columns), F32),
            pltpu.VMEM((tokens, rows_out), BF16),
            pltpu.VMEM((rows_out, width), BF16),
            pltpu.VMEM((outer, inner, block, width), F32),
            pltpu.VMEM((outer, inner, block, width), BF16),
            pltpu.VMEM((inner, outer, block, width), BF16),
            pltpu.VMEM((outer, block, width), BF16),
            pltpu.VMEM((outer, block, width), BF16),
            pltpu.VMEM((wide, block, width), BF16),
            pltpu.VMEM((half, columns), BF16),
            pltpu.VMEM((half, columns), BF16),
            pltpu.VMEM((half, columns), BF16),
            pltpu.VMEM((cross, half, columns), BF16),
            pltpu.VMEM((2, half, columns), BF16),
            dma((2,)),
            dma((2,)),
            dma((chunks,)),
            dma((wide,)),
            dma((wide,)),
            dma((chunks, outer)),
            dma((chunks, outer)),
            dma((chunks, inner, outer)),
            dma((chunks, inner, outer)),
            dma((outer,)),
            dma((outer,)),
            dma((inner, outer)),
            dma((inner, outer)),
            dma((inner,)),
            dma((inner,)),
            dma((outer,)),
            dma((outer,)),
            dma,
            dma,
            dma((cross,)),
            dma((cross,)),
            dma,
            dma,
        ],
        compiler_params=pltpu.CompilerParams(
            collective_id=0, has_side_effects=True, vmem_limit_bytes=VMEM_LIMIT
        ),
        name="rotate",
    )(activations, out_grads, basis_in, basis_out)
    return grads.reshape(tokens, width), acts.reshape(tokens, columns)


def mix_kernel(docs, grads, acts, eigenvalues, queries, ids, out, lanes):
    j = pl.program_id(0)

    @pl.when(j == 0)
    def _():
        lanes[...] = jnp.zeros_like(lanes)

    scale = 1.0 / (eigenvalues[...].astype(F32) + DAMPING)
    acts_float = acts[...].astype(F32)
    for q in range(queries.shape[0]):
        precond = (queries[q].astype(F32) * scale).astype(BF16)
        mixed = jnp.dot(grads[...], precond, preferred_element_type=F32) * acts_float
        part = mixed[:, :128]
        for k in range(1, mixed.shape[1] // 128):
            part = part + mixed[:, k * 128 : (k + 1) * 128]
        lanes[q] += part

    @pl.when(j == pl.num_programs(0) - 1)
    def _():
        tokens = lanes.shape[1]
        member = (ids[...] == lax.broadcasted_iota(jnp.int32, (docs, tokens), 0)).astype(F32)
        for q in range(queries.shape[0]):
            out[q] = jnp.dot(member, lanes[q], precision=lax.Precision.HIGHEST, preferred_element_type=F32)


def mix(docs, rot_grads, rot_acts, eigenvalues, queries, doc_ids):
    tokens, width = rot_grads.shape
    count, _, columns = queries.shape
    tile = tile_of(columns, 256)
    return pl.pallas_call(
        functools.partial(mix_kernel, docs),
        grid=(columns // tile,),
        out_shape=jax.ShapeDtypeStruct((count, docs, 128), F32),
        in_specs=[
            pl.BlockSpec((tokens, width), lambda j: (0, 0)),
            pl.BlockSpec((tokens, tile), lambda j: (0, j)),
            pl.BlockSpec((width, tile), lambda j: (0, j)),
            pl.BlockSpec((count, width, tile), lambda j: (0, 0, j)),
            pl.BlockSpec((1, tokens), lambda j: (0, 0)),
        ],
        out_specs=pl.BlockSpec((count, docs, 128), lambda j: (0, 0, 0)),
        scratch_shapes=[pltpu.VMEM((count, tokens, 128), F32)],
        compiler_params=pltpu.CompilerParams(vmem_limit_bytes=VMEM_LIMIT),
        name="mix",
    )(rot_grads, rot_acts, eigenvalues, queries, doc_ids.reshape(1, tokens))


def add_kernel(wide, narrow, part, out, held, across, send_w, recv_w, send_n, recv_n):
    w, n = lax.axis_index("wide"), lax.axis_index("narrow")
    greet(wide, narrow)

    def over_narrow(d):
        return remote(
            part, across.at[n], send_n.at[d], recv_n.at[d], {"narrow": lax.rem(n + d, narrow)}
        )

    def over_wide(d):
        return remote(
            held.at[w], held.at[w], send_w.at[d], recv_w.at[d], {"wide": lax.rem(w + d, wide)}
        )

    for d in range(1, narrow):
        over_narrow(d).start()
    across[n] = part[...]
    for d in range(1, narrow):
        over_narrow(d).wait_recv()
    value = across[0]
    for d in range(1, narrow):
        value = value + across[d]
    held[w] = value
    for d in range(1, wide):
        over_wide(d).start()
    for d in range(1, wide):
        over_wide(d).wait_recv()
    value = held[0]
    for d in range(1, wide):
        value = value + held[d]
    sums = jnp.sum(value, axis=2)
    for q in range(part.shape[0]):
        out[q : q + 1, :] = sums[q : q + 1, :]
    for d in range(1, narrow):
        over_narrow(d).wait_send()
    for d in range(1, wide):
        over_wide(d).wait_send()


def add_up(wide, narrow, part):
    dma = pltpu.SemaphoreType.DMA
    return pl.pallas_call(
        functools.partial(add_kernel, wide, narrow),
        out_shape=jax.ShapeDtypeStruct(part.shape[:2], F32),
        in_specs=[pl.BlockSpec(memory_space=pltpu.VMEM)],
        out_specs=pl.BlockSpec(memory_space=pltpu.VMEM),
        scratch_shapes=[
            pltpu.VMEM((wide,) + part.shape, F32),
            pltpu.VMEM((narrow,) + part.shape, F32),
            dma((wide,)),
            dma((wide,)),
            dma((narrow,)),
            dma((narrow,)),
        ],
        compiler_params=pltpu.CompilerParams(collective_id=1, has_side_effects=True),
        name="add_up",
    )(part)


def solution(mesh):
    wide, narrow = mesh.shape["wide"], mesh.shape["narrow"]

    def shards(activations, out_grads, basis_in, basis_out, eigenvalues, queries, doc_ids):
        rot_grads, rot_acts = rotate(wide, narrow, activations, out_grads, basis_in, basis_out)
        part = mix(DOC_PER * wide, rot_grads, rot_acts, eigenvalues, queries, doc_ids)
        return add_up(wide, narrow, part).T

    return jax.shard_map(
        shards,
        mesh=mesh,
        in_specs=(
            P("wide", "narrow"),
            P("wide", None),
            P("narrow", "wide"),
            P("wide", "narrow"),
            P("narrow", "wide"),
            P(None, "narrow", "wide"),
            P(),
        ),
        out_specs=P(),
        check_vma=False,
    )
```

time: 314 us -> 139 us (0.44)
  blocking collectives: 214 us -> 0 us
  Pallas kernels: 0 us -> 138 us
  matrix products: 49.2 us -> 0 us
  other arithmetic: 16.8 us -> 0 us
  between operations: 13.4 us -> 0.02 us
  waiting for transfers between devices: 7.82 us -> 0 us
  starting transfers between devices: 7.31 us -> 0 us
  local copies, waits for them, and re-layouts: 4.67 us -> 1.22 us
    psum x3 -> x0, blocking collectives: 214 us -> none  [the longest x1 110 us: shards(): rot_grads = lax.psum(partial_grads, 'wide').astype(jnp.bfloat16)]
    pallas_call x0 -> x3, Pallas kernels: none -> 138 us  [the longest x1 100 us: rotate(): pl.pallas_call(functools.partial(rotate_kernel, wide, narrow), out_shape=...]
    dot_general x4 -> x0, matrix products: 49.2 us -> none  [the longest x1 24.1 us: shards(): jnp.dot(lax.all_gather(activations, 'wide', axis=0, tiled=True), basis_in...]
    add x1 -> x0, other arithmetic: 16.8 us -> none  [shards(): eigenvalues.astype(jnp.float32)[None] + DAMPING]
    all_to_all x1 -> x0, starting transfers between devices: 7.31 us -> none  [shards(): lax.all_to_all(out_grads, 'wide', split_axis=1, concat_axis=0, tiled=True)]
    all_to_all x1 -> x0, waiting for transfers between devices: 7.09 us -> none  [shards(): lax.all_to_all(out_grads, 'wide', split_axis=1, concat_axis=0, tiled=True)]
  transfers between devices with their start and end apart: 2 -> 0, of which waited for: 1 -> 0; matrix products, arithmetic and copies ran while one was open for 7% -> 0% of each run, Pallas kernels for 0% -> 0%
where the time goes in v1:
time: 139 us
  Pallas kernels  138 us (99%)
    pallas_call x1, Pallas kernels, rotate(): pl.pallas_call(functools.partial(rotate_kernel, wide, narrow), out_shape=...  100 us
    pallas_call x1, Pallas kernels, mix(): pl.pallas_call(functools.partial(mix_kernel, docs), grid=(columns // tile...  22.9 us
    pallas_call x1, Pallas kernels, add_up(): pl.pallas_call(functools.partial(add_kernel, wide, narrow), out_shape=jax...  14.6 us

profile of v1, /device:TPU:0, one launch (start us, length us, event | category | flops | bytes accessed | tf_op | source)
XLA Modules:
  0.0 138.8 jit_solution(566728599948461276)
XLA Ops:
  0.0 100.1 %rotate.1 = (bf16[8,32,2048]{2,1,0:T(8,128)(2,1)}, bf16[2,128,3584]{2,1,0:T(8,128)(2,1)}) custom-call(bf16[32,7168]{1,0:T(8,128)(2,1)} %acts.1, bf16[32,8192]{1,0:T(8,128)(2,1)} %grads.1, bf16[7168,3584]{1,0:T(8,128)(2,1)} %basis_in.1, bf16[1024,2048]{1,0:T(8,128)(2,1)} %basis_out.1), custom_call_target="tpu_custom_call" | custom-call | tf_op jit(solution)/shard_map/rotate/pallas_call | solution.py:354
  100.1 22.9 %mix.1.part = f32[2,16,128]{2,1,0:T(8,128)} custom-call(bf16[256,2048]{1,0:T(8,128)(2,1)} %bitcast.5, bf16[256,3584]{1,0:T(8,128)(2,1)} %bitcast.4, bf16[2048,3584]{1,0:T(8,128)(2,1)} %eigenvalues.1, bf16[2,2048,3584]{2,1,0:T(8,128)(2,1)} %queries.1, s32[1,256]{1,0:T(1,128)} %bitcast.7), custom_call_target="tpu_custom_call" | custom-call | tf_op jit(solution)/shard_map/mix/pallas_call | solution.py:440
  123.0 14.6 %add_up.1 = f32[2,16]{1,0:T(2,128)} custom-call(f32[2,16,128]{2,1,0:T(8,128)} %mix.1.part), custom_call_target="tpu_custom_call" | custom-call | tf_op jit(solution)/shard_map/add_up/pallas_call | solution.py:499
  137.6 1.2 copy.9

commit v2 on v1

v2 whole, which is shorter than its diff:
```python
import functools

import jax
import jax.numpy as jnp
from jax import lax
from jax.experimental import pallas as pl
from jax.experimental.pallas import tpu as pltpu
from jax.sharding import PartitionSpec as P

DOC_PER = 2
DAMPING = 0.1
F32 = jnp.float32
BF16 = jnp.bfloat16
ANY = pl.BlockSpec(memory_space=pl.ANY)
VMEM_LIMIT = 67_043_328


def tile_of(size, most):
    return max(t for t in range(128, most + 1, 128) if size % t == 0)


def grid_of(wide):
    outer = max(o for o in (1, 2, 3, 4) if wide % o == 0)
    return outer, wide // outer


def remote(src, dst, send, recv, device):
    return pltpu.make_async_remote_copy(
        src_ref=src,
        dst_ref=dst,
        send_sem=send,
        recv_sem=recv,
        device_id=device,
        device_id_type=pl.DeviceIdType.MESH,
    )


def greet(wide, narrow):
    w, n = lax.axis_index("wide"), lax.axis_index("narrow")
    barrier = pltpu.get_barrier_semaphore()
    for d in range(1, wide):
        pl.semaphore_signal(
            barrier, inc=1, device_id={"wide": lax.rem(w + d, wide)}, device_id_type=pl.DeviceIdType.MESH
        )
    for d in range(1, narrow):
        pl.semaphore_signal(
            barrier, inc=1, device_id={"narrow": lax.rem(n + d, narrow)}, device_id_type=pl.DeviceIdType.MESH
        )
    pl.semaphore_wait(barrier, wide + narrow - 2)


def score_kernel(
    wide, narrow, docs, acts, grads, basis_in, basis_out, eigenvalues, queries, ids, out, precond,
    acts_all, weights, total, rows_held, weights_out, grads_part, grads_send, first_recv, second_send,
    second_recv, grads_all, acts_send, core_recv, cross_send, cross_recv, acts_done,
    eig_tile, query_tile, pre_tile, mix_tile, mixed, lanes, held, across,
    local_sem, weight_sem, out_sem, eig_sem, query_sem, put_sem, get_sem, a2a_s, a2a_r,
    line_s, line_r, side_s, side_r, gline_s, gline_r, gside_s, gside_r,
    first_s, first_r, second_s, second_r, core_s, core_r, cross_s, cross_r, done_s, done_r, last_s, last_r,
    send_w, recv_w, send_n, recv_n,
):
    outer, inner = grid_of(wide)
    cross = narrow // 2
    w, n = lax.axis_index("wide"), lax.axis_index("narrow")
    wo, wi = w // inner, lax.rem(w, inner)
    nx, nc = n // 2, lax.rem(n, 2)
    chunks, tokens, depth = acts_all.shape
    block = acts.shape[0]
    columns = total.shape[1]
    rows_out = basis_out.shape[0]
    half = tokens // 2

    def line_peer(d):
        return {"wide": lax.rem(wo + d, outer) * inner + wi}

    def side_peer(e):
        return {"wide": wo * inner + lax.rem(wi + e, inner)}

    def cut(c):
        return pl.ds(pl.multiple_of(c * depth, 128), depth)

    def rows(source):
        return pl.ds(pl.multiple_of(source * block, block), block)

    def line_source(d):
        return lax.rem(wo + outer - d, outer) * inner + wi

    def weight(c):
        slot = lax.rem(c, 2)
        return pltpu.make_async_copy(
            basis_in.at[pl.ds(pl.multiple_of(c * depth, 128), depth)], weights.at[slot], weight_sem.at[slot]
        )

    fetch_out = pltpu.make_async_copy(basis_out, weights_out, local_sem.at[0])
    own_rows = pltpu.make_async_copy(
        grads.at[:, pl.ds(pl.multiple_of(w * rows_out, 128), rows_out)], rows_held.at[rows(w)], local_sem.at[1]
    )

    def own_acts(c):
        return pltpu.make_async_copy(acts.at[:, cut(c)], acts_all.at[c, rows(w)], out_sem.at[c])

    own_rows.start()
    fetch_out.start()
    for c in range(chunks):
        own_acts(c).start()
    weight(0).start()
    weight(1).start()
    count, width, _ = queries.shape
    slab = eig_tile.shape[1]
    slabs = width // slab

    def slab_rows(k):
        return pl.ds(pl.multiple_of(k * slab, 16), slab)

    def eig_copy(k):
        slot = lax.rem(k, 2)
        return pltpu.make_async_copy(eigenvalues.at[slab_rows(k)], eig_tile.at[slot], eig_sem.at[slot])

    def query_copy(k):
        slot = lax.rem(k, 2)
        return pltpu.make_async_copy(queries.at[:, slab_rows(k)], query_tile.at[slot], query_sem.at[slot])

    def put_copy(k):
        slot = lax.rem(k, 2)
        return pltpu.make_async_copy(pre_tile.at[slot], precond.at[:, slab_rows(k)], put_sem.at[slot])

    for k in range(2):
        eig_copy(k).start()
        query_copy(k).start()
    greet(wide, narrow)

    def swap(d):
        to = lax.rem(w + d, wide)
        return remote(
            grads.at[:, pl.ds(pl.multiple_of(to * rows_out, 128), rows_out)],
            rows_held.at[rows(w)],
            a2a_s.at[d],
            a2a_r.at[d],
            {"wide": to},
        )

    def line_copy(c, d):
        return remote(
            acts.at[:, cut(c)], acts_all.at[c, rows(w)], line_s.at[c, d], line_r.at[c, d], line_peer(d)
        )

    def side_own(c, e):
        return remote(
            acts.at[:, cut(c)], acts_all.at[c, rows(w)], side_s.at[c, e, 0], side_r.at[c, e, 0], side_peer(e)
        )

    def side_pass(c, e, d):
        source = line_source(d)
        return remote(
            acts_all.at[c, rows(source)],
            acts_all.at[c, rows(source)],
            side_s.at[c, e, d],
            side_r.at[c, e, d],
            side_peer(e),
        )

    def begin(c, carry):
        for d in range(1, outer):
            line_copy(c, d).start()
        for e in range(1, inner):
            side_own(c, e).start()
        return carry

    early = (chunks + 1) // 3
    middle = (2 * chunks) // 3
    lax.fori_loop(0, early, begin, 0)
    for d in range(1, wide):
        swap(d).start()
    lax.fori_loop(early, chunks, begin, 0)
    wt = tile_of(width, 512)

    def grads_tile(k, carry):
        at = pl.ds(pl.multiple_of(k * wt, 128), wt)
        part = jnp.dot(rows_held[...], weights_out[:, at], preferred_element_type=F32)
        part = part.reshape(outer, inner, block, wt)
        grads_part[:, :, :, at] = part
        grads_send[:, :, :, at] = part.astype(BF16)
        return carry

    def first(e):
        return remote(
            grads_send.at[:, lax.rem(wi + e, inner)], first_recv.at[e], first_s.at[e], first_r.at[e], side_peer(e)
        )

    def second(d):
        return remote(
            second_send.at[lax.rem(wo + d, outer)], second_recv.at[d], second_s.at[d], second_r.at[d], line_peer(d)
        )

    ct = tile_of(columns, 512)

    def forward(c):
        for d in range(1, outer):
            line_copy(c, d).wait_recv()
            for e in range(1, inner):
                side_pass(c, e, d).start()

    ps = tile_of(columns, 512)

    def condition(k):
        slot = lax.rem(k, 2)
        eig_copy(k).wait()
        query_copy(k).wait()

        @pl.when(k >= 2)
        def _():
            put_copy(k - 2).wait()

        def piece(m, carry):
            at = pl.ds(pl.multiple_of(m * ps, 128), ps)
            scale = 1.0 / (eig_tile[slot, :, at].astype(F32) + DAMPING)
            for q in range(count):
                pre_tile[slot, q, :, at] = (query_tile[slot, q, :, at].astype(F32) * scale).astype(BF16)
            return carry

        lax.fori_loop(0, columns // ps, piece, 0)
        put_copy(k).start()

        @pl.when(k + 2 < slabs)
        def _():
            eig_copy(k + 2).start()
            query_copy(k + 2).start()

    each = pl.cdiv(slabs, chunks)

    def step(c, carry):
        def slab_step(m, inside):
            @pl.when(c * each + m < slabs)
            def _():
                condition(c * each + m)

            return inside

        @pl.when(c + 1 < chunks)
        def _():
            forward(c + 1)

        own_acts(c).wait()
        for e in range(1, inner):
            side_own(c, e).wait_recv()
            for d in range(1, outer):
                side_pass(c, e, d).wait_recv()
        weight(c).wait()
        slot = lax.rem(c, 2)

        def tile(k, carry):
            at = pl.ds(pl.multiple_of(k * ct, 128), ct)
            part = jnp.dot(acts_all[c], weights[slot, :, at], preferred_element_type=F32)

            @pl.when(c == 0)
            def _():
                total[:, at] = part

            @pl.when(c > 0)
            def _():
                total[:, at] += part

            return carry

        lax.fori_loop(0, columns // ct, tile, 0)

        @pl.when(c + 2 < chunks)
        def _():
            weight(c + 2).start()

        lax.fori_loop(0, each, slab_step, 0)

        return carry

    forward(0)
    lax.fori_loop(0, early, step, 0)
    own_rows.wait()
    fetch_out.wait()
    for d in range(1, wide):
        swap(d).wait_recv()
    lax.fori_loop(0, width // wt, grads_tile, 0)
    for e in range(1, inner):
        first(e).start()
    lax.fori_loop(early, middle, step, 0)
    for e in range(1, inner):
        first(e).wait_recv()
    for o in range(outer):
        value = grads_part[o, wi]
        for e in range(1, inner):
            value = value + first_recv[e, o].astype(F32)
        second_send[o] = value
    for d in range(1, outer):
        second(d).start()
    lax.fori_loop(middle, chunks, step, 0)

    share = half // cross

    def to_send(k, carry):
        at = pl.ds(pl.multiple_of(k * ct, 128), ct)
        acts_send[:, at] = total[pl.ds(pl.multiple_of((1 - nc) * half, half), half), at]
        return carry

    lax.fori_loop(0, columns // ct, to_send, 0)
    partner = {"narrow": nx * 2 + (1 - nc)}

    def cross_peer(d):
        return {"narrow": lax.rem(nx + d, cross) * 2 + nc}

    core_copy = remote(acts_send, core_recv, core_s, core_r, partner)
    core_copy.start()

    for k in range(min(2, slabs)):
        put_copy(slabs - 1 - k).wait()
    jt = mix_tile.shape[3]
    tiles = columns // jt

    def get_copy(j):
        slot = lax.rem(j, 2)
        return pltpu.make_async_copy(
            precond.at[:, :, pl.ds(pl.multiple_of(j * jt, 128), jt)], mix_tile.at[slot], get_sem.at[slot]
        )

    for j in range(2):
        get_copy(j).start()

    core_copy.wait_recv()

    def core_sum(k, carry):
        at = pl.ds(pl.multiple_of(k * ct, 128), ct)
        value = total[pl.ds(pl.multiple_of(nc * half, half), half), at] + core_recv[:, at]
        for x in range(cross):
            cross_send[x, :, at] = value[x * share : (x + 1) * share]
        return carry

    lax.fori_loop(0, columns // ct, core_sum, 0)

    def cross_copy(d):
        return remote(
            cross_send.at[lax.rem(nx + d, cross)], cross_recv.at[d], cross_s.at[d], cross_r.at[d], cross_peer(d)
        )

    for d in range(1, cross):
        cross_copy(d).start()

    for d in range(1, outer):
        second(d).wait_recv()
    value = second_send[wo]
    for d in range(1, outer):
        value = value + second_recv[d]
    grads_all[w] = value.astype(BF16)

    def gline(d):
        return remote(grads_all.at[w], grads_all.at[w], gline_s.at[d], gline_r.at[d], line_peer(d))

    def gside(e, d):
        source = line_source(d)
        return remote(
            grads_all.at[source], grads_all.at[source], gside_s.at[e, d], gside_r.at[e, d], side_peer(e)
        )

    for d in range(1, outer):
        gline(d).start()
    for e in range(1, inner):
        gside(e, 0).start()
    for d in range(1, outer):
        gline(d).wait_recv()
        for e in range(1, inner):
            gside(e, d).start()
    for e in range(1, inner):
        for d in range(outer):
            gside(e, d).wait_recv()

    def mix(j, carry):
        slot = lax.rem(j, 2)
        get_copy(j).wait()
        left = grads_all[...].reshape(tokens, width)
        at = pl.ds(pl.multiple_of(j * jt, 128), jt)
        for q in range(count):
            mixed[q, :, at] = jnp.dot(left, mix_tile[slot, q], preferred_element_type=F32)

        @pl.when(j + 2 < tiles)
        def _():
            get_copy(j + 2).start()

        return carry

    first_part = tiles // 4
    second_part = (3 * tiles) // 4
    lax.fori_loop(0, first_part, mix, 0)
    for d in range(1, cross):
        cross_copy(d).wait_recv()

    def cross_sum(k, carry):
        at = pl.ds(pl.multiple_of(k * ct, 128), ct)
        value = cross_send[nx, :, at]
        for d in range(1, cross):
            value = value + cross_recv[d, :, at]
        acts_done[nc, nx, :, at] = value.astype(BF16)
        return carry

    lax.fori_loop(0, columns // ct, cross_sum, 0)

    def done_copy(d):
        return remote(acts_done.at[nc, nx], acts_done.at[nc, nx], done_s.at[d], done_r.at[d], cross_peer(d))

    def last_copy(d):
        x = lax.rem(nx + cross - d, cross)
        return remote(acts_done.at[nc, x], acts_done.at[nc, x], last_s.at[d], last_r.at[d], partner)

    for d in range(1, cross):
        done_copy(d).start()
    last_copy(0).start()
    lax.fori_loop(first_part, second_part, mix, 0)
    for d in range(1, cross):
        done_copy(d).wait_recv()
        last_copy(d).start()
    lax.fori_loop(second_part, tiles, mix, 0)
    for d in range(cross):
        last_copy(d).wait_recv()

    lanes[...] = jnp.zeros_like(lanes)

    def fold(j, carry):
        at = pl.ds(pl.multiple_of(j * 128, 128), 128)
        right = acts_done[:, :, :, at].reshape(tokens, 128).astype(F32)
        for q in range(count):
            lanes[q] += mixed[q, :, at] * right
        return carry

    lax.fori_loop(0, columns // 128, fold, 0)
    _, rows_pad, docs_pad = across.shape
    member = (ids[...] == lax.broadcasted_iota(jnp.int32, (docs_pad, tokens), 0)).astype(F32)
    row = lax.broadcasted_iota(jnp.int32, (rows_pad, docs_pad), 0)
    value = jnp.zeros((rows_pad, docs_pad), F32)
    for q in range(count):
        doc_lanes = jnp.dot(member, lanes[q], precision=lax.Precision.HIGHEST, preferred_element_type=F32)
        value = jnp.where(row == q, jnp.sum(doc_lanes, axis=1)[None, :], value)
    across[n] = value

    def over_narrow(d):
        return remote(across.at[n], across.at[n], send_n.at[d], recv_n.at[d], {"narrow": lax.rem(n + d, narrow)})

    def over_wide(d):
        return remote(held.at[w], held.at[w], send_w.at[d], recv_w.at[d], {"wide": lax.rem(w + d, wide)})

    for d in range(1, narrow):
        over_narrow(d).start()
    for d in range(1, narrow):
        over_narrow(d).wait_recv()
    value = across[0]
    for d in range(1, narrow):
        value = value + across[d]
    held[w] = value
    for d in range(1, wide):
        over_wide(d).start()
    for d in range(1, wide):
        over_wide(d).wait_recv()
    value = held[0]
    for d in range(1, wide):
        value = value + held[d]
    out[...] = value[: out.shape[0], : out.shape[1]]

    for d in range(1, wide):
        swap(d).wait_send()

    def drain(c, carry):
        for d in range(1, outer):
            line_copy(c, d).wait_send()
        for e in range(1, inner):
            side_own(c, e).wait_send()
            for d in range(1, outer):
                side_pass(c, e, d).wait_send()
        return carry

    lax.fori_loop(0, chunks, drain, 0)
    for e in range(1, inner):
        first(e).wait_send()
        for d in range(outer):
            gside(e, d).wait_send()
    for d in range(1, outer):
        second(d).wait_send()
        gline(d).wait_send()
    core_copy.wait_send()
    for d in range(1, cross):
        cross_copy(d).wait_send()
        done_copy(d).wait_send()
    for d in range(cross):
        last_copy(d).wait_send()
    for d in range(1, narrow):
        over_narrow(d).wait_send()
    for d in range(1, wide):
        over_wide(d).wait_send()


def score(wide, narrow, activations, out_grads, basis_in, basis_out, eigenvalues, queries, doc_ids):
    outer, inner = grid_of(wide)
    cross = narrow // 2
    block, depth_all = activations.shape
    tokens = block * wide
    docs = DOC_PER * wide
    depth = tile_of(depth_all, 1024)
    chunks = depth_all // depth
    columns = basis_in.shape[1]
    rows_out, width = basis_out.shape
    count = queries.shape[0]
    half = tokens // 2
    slab = tile_of(width, 128) // 2
    jt = tile_of(columns, 256)
    rows_pad, docs_pad = pl.cdiv(count, 8) * 8, pl.cdiv(docs, 128) * 128
    dma = pltpu.SemaphoreType.DMA
    scores, _ = pl.pallas_call(
        functools.partial(score_kernel, wide, narrow, docs),
        out_shape=(
            jax.ShapeDtypeStruct((count, docs), F32),
            jax.ShapeDtypeStruct((count, width, columns), BF16),
        ),
        in_specs=[ANY] * 6 + [pl.BlockSpec(memory_space=pltpu.VMEM)],
        out_specs=(pl.BlockSpec(memory_space=pltpu.VMEM), ANY),
        scratch_shapes=[
            pltpu.VMEM((chunks, tokens, depth), BF16),
            pltpu.VMEM((2, depth, columns), BF16),
            pltpu.VMEM((tokens, columns), F32),
            pltpu.VMEM((tokens, rows_out), BF16),
            pltpu.VMEM((rows_out, width), BF16),
            pltpu.VMEM((outer, inner, block, width), F32),
            pltpu.VMEM((outer, inner, block, width), BF16),
            pltpu.VMEM((inner, outer, block, width), BF16),
            pltpu.VMEM((outer, block, width), F32),
            pltpu.VMEM((outer, block, width), F32),
            pltpu.VMEM((wide, block, width), BF16),
            pltpu.VMEM((half, columns), F32),
            pltpu.VMEM((half, columns), F32),
            pltpu.VMEM((cross, half // cross, columns), F32),
            pltpu.VMEM((cross, half // cross, columns), F32),
            pltpu.VMEM((2, cross, half // cross, columns), BF16),
            pltpu.VMEM((2, slab, columns), BF16),
            pltpu.VMEM((2, count, slab, columns), BF16),
            pltpu.VMEM((2, count, slab, columns), BF16),
            pltpu.VMEM((2, count, width, jt), BF16),
            pltpu.VMEM((count, tokens, columns), F32),
            pltpu.VMEM((count, tokens, 128), F32),
            pltpu.VMEM((wide, rows_pad, docs_pad), F32),
            pltpu.VMEM((narrow, rows_pad, docs_pad), F32),
            dma((2,)),
            dma((2,)),
            dma((chunks,)),
            dma((2,)),
            dma((2,)),
            dma((2,)),
            dma((2,)),
            dma((wide,)),
            dma((wide,)),
            dma((chunks, outer)),
            dma((chunks, outer)),
            dma((chunks, inner, outer)),
            dma((chunks, inner, outer)),
            dma((outer,)),
            dma((outer,)),
            dma((inner, outer)),
            dma((inner, outer)),
            dma((inner,)),
            dma((inner,)),
            dma((outer,)),
            dma((outer,)),
            dma,
            dma,
            dma((cross,)),
            dma((cross,)),
            dma((cross,)),
            dma((cross,)),
            dma((cross,)),
            dma((cross,)),
            dma((wide,)),
            dma((wide,)),
            dma((narrow,)),
            dma((narrow,)),
        ],
        compiler_params=pltpu.CompilerParams(
            collective_id=0, has_side_effects=True, vmem_limit_bytes=VMEM_LIMIT
        ),
        name="score",
    )(activations, out_grads, basis_in, basis_out, eigenvalues, queries, doc_ids.reshape(1, tokens))
    return scores.T


def solution(mesh):
    wide, narrow = mesh.shape["wide"], mesh.shape["narrow"]

    def shards(activations, out_grads, basis_in, basis_out, eigenvalues, queries, doc_ids):
        return score(
            wide, narrow, activations, out_grads, basis_in, basis_out, eigenvalues, queries, doc_ids
        )

    return jax.shard_map(
        shards,
        mesh=mesh,
        in_specs=(
            P("wide", "narrow"),
            P("wide", None),
            P("narrow", "wide"),
            P("wide", "narrow"),
            P("narrow", "wide"),
            P(None, "narrow", "wide"),
            P(),
        ),
        out_specs=P(),
        check_vma=False,
    )
```

time: 139 us -> 164 us (1.18)
  Pallas kernels: 138 us -> 162 us
    pallas_call x3 -> x1, Pallas kernels: 138 us -> 162 us  [score(): pl.pallas_call(functools.partial(score_kernel, wide, narrow, docs), out_s...]
where the time goes in v2:
time: 164 us; the launch traced here: 163 us
  Pallas kernels  162 us (99%)
    pallas_call x1, Pallas kernels, score(): pl.pallas_call(functools.partial(score_kernel, wide, narrow, docs), out_s...  162 us

profile of v2, /device:TPU:0, one launch (start us, length us, event | category | flops | bytes accessed | tf_op | source)
XLA Modules:
  0.0 163.0 jit_solution(3730242728831680183)
XLA Ops:
  0.0 161.8 %score.1 = (f32[2,16]{1,0:T(2,128)}, bf16[2,2048,3584]{2,1,0:T(8,128)(2,1)}) custom-call(bf16[32,7168]{1,0:T(8,128)(2,1)} %acts.1, bf16[32,8192]{1,0:T(8,128)(2,1)} %grads.1, bf16[7168,3584]{1,0:T(8,128)(2,1)} %basis_in.1, bf16[1024,2048]{1,0:T(8,128)(2,1)} %basis_out.1, bf16[2048,3584]{1,0:T(8,128)(2,1)} %eigenvalues.1, bf16[2,2048,3584]{2,1,0:T(8,128)(2,1)} %queries.1, ...), custom_call_target="tpu_custom_call" | custom-call | tf_op jit(solution)/shard_map/score/pallas_call | solution.py:511
  161.8 1.2 copy.9

commit v3 on v2

--- a/solution.py
+++ b/solution.py
@@ -50,11 +50,11 @@
 
 
 def score_kernel(
-    wide, narrow, docs, acts, grads, basis_in, basis_out, eigenvalues, queries, ids, out, precond,
+    wide, narrow, docs, acts, grads, basis_in, basis_out, eigenvalues, queries, ids, out,
     acts_all, weights, total, rows_held, weights_out, grads_part, grads_send, first_recv, second_send,
     second_recv, grads_all, acts_send, core_recv, cross_send, cross_recv, acts_done,
-    eig_tile, query_tile, pre_tile, mix_tile, mixed, lanes, held, across,
-    local_sem, weight_sem, out_sem, eig_sem, query_sem, put_sem, get_sem, a2a_s, a2a_r,
+    eig_tile, query_tile, mixed, lanes, held, across,
+    local_sem, weight_sem, out_sem, eig_sem, query_sem, a2a_s, a2a_r,
     line_s, line_r, side_s, side_r, gline_s, gline_r, gside_s, gside_r,
     first_s, first_r, second_s, second_r, core_s, core_r, cross_s, cross_r, done_s, done_r, last_s, last_r,
     send_w, recv_w, send_n, recv_n,
@@ -106,27 +106,20 @@
     weight(0).start()
     weight(1).start()
     count, width, _ = queries.shape
-    slab = eig_tile.shape[1]
-    slabs = width // slab
-
-    def slab_rows(k):
-        return pl.ds(pl.multiple_of(k * slab, 16), slab)
-
-    def eig_copy(k):
-        slot = lax.rem(k, 2)
-        return pltpu.make_async_copy(eigenvalues.at[slab_rows(k)], eig_tile.at[slot], eig_sem.at[slot])
-
-    def query_copy(k):
-        slot = lax.rem(k, 2)
-        return pltpu.make_async_copy(queries.at[:, slab_rows(k)], query_tile.at[slot], query_sem.at[slot])
-
-    def put_copy(k):
-        slot = lax.rem(k, 2)
-        return pltpu.make_async_copy(pre_tile.at[slot], precond.at[:, slab_rows(k)], put_sem.at[slot])
-
-    for k in range(2):
-        eig_copy(k).start()
-        query_copy(k).start()
+    jt = eig_tile.shape[2]
+    tiles = columns // jt
+
+    def mix_columns(j):
+        return pl.ds(pl.multiple_of(j * jt, 128), jt)
+
+    def eig_copy(j):
+        slot = lax.rem(j, 2)
+        return pltpu.make_async_copy(eigenvalues.at[:, mix_columns(j)], eig_tile.at[slot], eig_sem.at[slot])
+
+    def query_copy(j):
+        slot = lax.rem(j, 2)
+        return pltpu.make_async_copy(queries.at[:, :, mix_columns(j)], query_tile.at[slot], query_sem.at[slot])
+
     greet(wide, narrow)
 
     def swap(d):
@@ -166,12 +159,10 @@
             side_own(c, e).start()
         return carry
 
-    early = (chunks + 1) // 3
-    middle = (2 * chunks) // 3
-    lax.fori_loop(0, early, begin, 0)
+    middle = chunks // 2
     for d in range(1, wide):
         swap(d).start()
-    lax.fori_loop(early, chunks, begin, 0)
+    lax.fori_loop(0, middle + 1, begin, 0)
     wt = tile_of(width, 512)
 
     def grads_tile(k, carry):
@@ -200,42 +191,7 @@
             for e in range(1, inner):
                 side_pass(c, e, d).start()
 
-    ps = tile_of(columns, 512)
-
-    def condition(k):
-        slot = lax.rem(k, 2)
-        eig_copy(k).wait()
-        query_copy(k).wait()
-
-        @pl.when(k >= 2)
-        def _():
-            put_copy(k - 2).wait()
-
-        def piece(m, carry):
-            at = pl.ds(pl.multiple_of(m * ps, 128), ps)
-            scale = 1.0 / (eig_tile[slot, :, at].astype(F32) + DAMPING)
-            for q in range(count):
-                pre_tile[slot, q, :, at] = (query_tile[slot, q, :, at].astype(F32) * scale).astype(BF16)
-            return carry
-
-        lax.fori_loop(0, columns // ps, piece, 0)
-        put_copy(k).start()
-
-        @pl.when(k + 2 < slabs)
-        def _():
-            eig_copy(k + 2).start()
-            query_copy(k + 2).start()
-
-    each = pl.cdiv(slabs, chunks)
-
     def step(c, carry):
-        def slab_step(m, inside):
-            @pl.when(c * each + m < slabs)
-            def _():
-                condition(c * each + m)
-
-            return inside
-
         @pl.when(c + 1 < chunks)
         def _():
             forward(c + 1)
@@ -268,12 +224,8 @@
         def _():
             weight(c + 2).start()
 
-        lax.fori_loop(0, each, slab_step, 0)
-
-        return carry
-
-    forward(0)
-    lax.fori_loop(0, early, step, 0)
+        return carry
+
     own_rows.wait()
     fetch_out.wait()
     for d in range(1, wide):
@@ -281,7 +233,8 @@
     lax.fori_loop(0, width // wt, grads_tile, 0)
     for e in range(1, inner):
         first(e).start()
-    lax.fori_loop(early, middle, step, 0)
+    forward(0)
+    lax.fori_loop(0, middle, step, 0)
     for e in range(1, inner):
         first(e).wait_recv()
     for o in range(outer):
@@ -291,6 +244,10 @@
         second_send[o] = value
     for d in range(1, outer):
         second(d).start()
+    lax.fori_loop(middle + 1, chunks, begin, 0)
+    for j in range(2):
+        eig_copy(j).start()
+        query_copy(j).start()
     lax.fori_loop(middle, chunks, step, 0)
 
     share = half // cross
@@ -308,20 +265,6 @@
 
     core_copy = remote(acts_send, core_recv, core_s, core_r, partner)
     core_copy.start()
-
-    for k in range(min(2, slabs)):
-        put_copy(slabs - 1 - k).wait()
-    jt = mix_tile.shape[3]
-    tiles = columns // jt
-
-    def get_copy(j):
-        slot = lax.rem(j, 2)
-        return pltpu.make_async_copy(
-            precond.at[:, :, pl.ds(pl.multiple_of(j * jt, 128), jt)], mix_tile.at[slot], get_sem.at[slot]
-        )
-
-    for j in range(2):
-        get_copy(j).start()
 
     core_copy.wait_recv()
 
@@ -372,15 +315,18 @@
 
     def mix(j, carry):
         slot = lax.rem(j, 2)
-        get_copy(j).wait()
+        eig_copy(j).wait()
+        query_copy(j).wait()
         left = grads_all[...].reshape(tokens, width)
-        at = pl.ds(pl.multiple_of(j * jt, 128), jt)
+        scale = 1.0 / (eig_tile[slot].astype(F32) + DAMPING)
         for q in range(count):
-            mixed[q, :, at] = jnp.dot(left, mix_tile[slot, q], preferred_element_type=F32)
+            precond = (query_tile[slot, q].astype(F32) * scale).astype(BF16)
+            mixed[q, :, mix_columns(j)] = jnp.dot(left, precond, preferred_element_type=F32)
 
         @pl.when(j + 2 < tiles)
         def _():
-            get_copy(j + 2).start()
+            eig_copy(j + 2).start()
+            query_copy(j + 2).start()
 
         return carry
 
@@ -504,18 +450,14 @@
     rows_out, width = basis_out.shape
     count = queries.shape[0]
     half = tokens // 2
-    slab = tile_of(width, 128) // 2
     jt = tile_of(columns, 256)
     rows_pad, docs_pad = pl.cdiv(count, 8) * 8, pl.cdiv(docs, 128) * 128
     dma = pltpu.SemaphoreType.DMA
-    scores, _ = pl.pallas_call(
+    scores = pl.pallas_call(
         functools.partial(score_kernel, wide, narrow, docs),
-        out_shape=(
-            jax.ShapeDtypeStruct((count, docs), F32),
-            jax.ShapeDtypeStruct((count, width, columns), BF16),
-        ),
+        out_shape=jax.ShapeDtypeStruct((count, docs), F32),
         in_specs=[ANY] * 6 + [pl.BlockSpec(memory_space=pltpu.VMEM)],
-        out_specs=(pl.BlockSpec(memory_space=pltpu.VMEM), ANY),
+        out_specs=pl.BlockSpec(memory_space=pltpu.VMEM),
         scratch_shapes=[
             pltpu.VMEM((chunks, tokens, depth), BF16),
             pltpu.VMEM((2, depth, columns), BF16),
@@ -533,9 +475,7 @@
             pltpu.VMEM((cross, half // cross, columns), F32),
             pltpu.VMEM((cross, half // cross, columns), F32),
             pltpu.VMEM((2, cross, half // cross, columns), BF16),
-            pltpu.VMEM((2, slab, columns), BF16),
-            pltpu.VMEM((2, count, slab, columns), BF16),
-            pltpu.VMEM((2, count, slab, columns), BF16),
+            pltpu.VMEM((2, width, jt), BF16),
             pltpu.VMEM((2, count, width, jt), BF16),
             pltpu.VMEM((count, tokens, columns), F32),
             pltpu.VMEM((count, tokens, 128), F32),
@@ -544,8 +484,6 @@
             dma((2,)),
             dma((2,)),
             dma((chunks,)),
-            dma((2,)),
-            dma((2,)),
             dma((2,)),
             dma((2,)),
             dma((wide,)),

time: 164 us -> 158 us (0.963)
  Pallas kernels: 162 us -> 157 us
    pallas_call x1, Pallas kernels: 162 us -> 157 us  [score(): pl.pallas_call(functools.partial(score_kernel, wide, narrow, docs), out_s...]
where the time goes in v3:
time: 158 us
  Pallas kernels  157 us (99%)
    pallas_call x1, Pallas kernels, score(): pl.pallas_call(functools.partial(score_kernel, wide, narrow, docs), out_s...  157 us

profile of v3, /device:TPU:0, one launch (start us, length us, event | category | flops | bytes accessed | tf_op | source)
XLA Modules:
  0.0 157.9 jit_solution(11493428892066593239)
XLA Ops:
  0.0 156.6 %score.1 = f32[2,16]{1,0:T(2,128)} custom-call(bf16[32,7168]{1,0:T(8,128)(2,1)} %acts.1, bf16[32,8192]{1,0:T(8,128)(2,1)} %grads.1, bf16[7168,3584]{1,0:T(8,128)(2,1)} %basis_in.1, bf16[1024,2048]{1,0:T(8,128)(2,1)} %basis_out.1, bf16[2048,3584]{1,0:T(8,128)(2,1)} %eigenvalues.1, bf16[2,2048,3584]{2,1,0:T(8,128)(2,1)} %queries.1, s32[1,256]{1,0:T(1,128)} %bitcast.3), custom_call_target="tpu_custom_call" | custom-call | tf_op jit(solution)/shard_map/score/pallas_call | solution.py:456
  156.6 1.2 copy.9

commit v4 on v3

--- a/solution.py
+++ b/solution.py
@@ -162,7 +162,7 @@
     middle = chunks // 2
     for d in range(1, wide):
         swap(d).start()
-    lax.fori_loop(0, middle + 1, begin, 0)
+    lax.fori_loop(0, chunks, begin, 0)
     wt = tile_of(width, 512)
 
     def grads_tile(k, carry):
@@ -241,10 +241,10 @@
         value = grads_part[o, wi]
         for e in range(1, inner):
             value = value + first_recv[e, o].astype(F32)
-        second_send[o] = value
+        grads_part[o, wi] = value
+        second_send[o] = value.astype(BF16)
     for d in range(1, outer):
         second(d).start()
-    lax.fori_loop(middle + 1, chunks, begin, 0)
     for j in range(2):
         eig_copy(j).start()
         query_copy(j).start()
@@ -287,9 +287,9 @@
 
     for d in range(1, outer):
         second(d).wait_recv()
-    value = second_send[wo]
+    value = grads_part[wo, wi]
     for d in range(1, outer):
-        value = value + second_recv[d]
+        value = value + second_recv[d].astype(F32)
     grads_all[w] = value.astype(BF16)
 
     def gline(d):
@@ -467,8 +467,8 @@
             pltpu.VMEM((outer, inner, block, width), F32),
             pltpu.VMEM((outer, inner, block, width), BF16),
             pltpu.VMEM((inner, outer, block, width), BF16),
-            pltpu.VMEM((outer, block, width), F32),
-            pltpu.VMEM((outer, block, width), F32),
+            pltpu.VMEM((outer, block, width), BF16),
+            pltpu.VMEM((outer, block, width), BF16),
             pltpu.VMEM((wide, block, width), BF16),
             pltpu.VMEM((half, columns), F32),
             pltpu.VMEM((half, columns), F32),

time: 158 us -> 130 us (0.82)
  Pallas kernels: 157 us -> 128 us
    pallas_call x1, Pallas kernels: 157 us -> 128 us  [score(): pl.pallas_call(functools.partial(score_kernel, wide, narrow, docs), out_s...]
where the time goes in v4:
time: 130 us
  Pallas kernels  128 us (98%)
    pallas_call x1, Pallas kernels, score(): pl.pallas_call(functools.partial(score_kernel, wide, narrow, docs), out_s...  128 us

profile of v4, /device:TPU:0, one launch (start us, length us, event | category | flops | bytes accessed | tf_op | source)
XLA Modules:
  0.0 129.6 jit_solution(1635181325944646840)
XLA Ops:
  0.0 128.4 %score.1 = f32[2,16]{1,0:T(2,128)} custom-call(bf16[32,7168]{1,0:T(8,128)(2,1)} %acts.1, bf16[32,8192]{1,0:T(8,128)(2,1)} %grads.1, bf16[7168,3584]{1,0:T(8,128)(2,1)} %basis_in.1, bf16[1024,2048]{1,0:T(8,128)(2,1)} %basis_out.1, bf16[2048,3584]{1,0:T(8,128)(2,1)} %eigenvalues.1, bf16[2,2048,3584]{2,1,0:T(8,128)(2,1)} %queries.1, s32[1,256]{1,0:T(1,128)} %bitcast.3), custom_call_target="tpu_custom_call" | custom-call | tf_op jit(solution)/shard_map/score/pallas_call | solution.py:456
  128.4 1.2 copy.9
